TPU v7x, 128 devices: a whole 4x4x4 slice. The times are simulated.
128 devices in a mesh: row: 8 (over y, core), col: 16 (over x, z).
Axes of the slice: x: 4, y: 4, z: 4, core: 2. Of those that a mesh axis runs over, the one named last changes fastest.
Arguments:
- scores: float32 [32, 98304], P(None, ('row', 'col')), may hold values from -60 to 60
- tile_values: bfloat16 [8, 16, 480, 128, 128], P('row', 'col'), may hold values from 0 to 1
- tile_rows: int32 [8, 16, 480], P('row', 'col'), may hold values from 0 to 95, as said below
- tile_cols: int32 [8, 16, 480], P('row', 'col'), may hold values from 0 to 47, as said below
- tile_count: int32 [8, 16], P('row', 'col'), may hold values from 240 to 480, as said below
Outputs:
- solution: float32 [32, 98304], P(None, ('row', 'col'))
- residual: float32 [32, 98304], P(None, ('row', 'col'))
Inputs may be any that keep to these rules, and one draw needn't show every extreme that they name: `tile_rows`: on every device each local row tile is named by exactly 5 of the 480 slots. `tile_cols`: on every device each local column tile is named by exactly 10 of the slots. Only the first tile_count slots of a device are live; some device has all 480 slots live.
All inputs are finite; a program needn't handle non-finite values.
Results may differ from a plain program's by a relative error of at most 0.0031.
Values may be sent and summed in bfloat16 or wider, within the bound.
A program may use at most 128 MiB of HBM per device.

v0:
```python
import jax
import jax.numpy as jnp
from jax import lax
from jax.sharding import PartitionSpec as P

PER_ROW = 5
ITERS = 3
coupling = 0.2


def per_device(scores, tile_values, tile_rows, tile_cols, tile_count):
    tile_blocks = tile_values[0, 0]
    row_tile_ids = tile_rows[0, 0]
    col_tile_ids = tile_cols[0, 0]
    live_count = tile_count[0, 0]
    slot_count = tile_blocks.shape[0]
    tile_size = tile_blocks.shape[1]
    task_count = scores.shape[0]
    piece_len = scores.shape[1]
    row_span = piece_len * lax.axis_size("col")
    col_span = piece_len * lax.axis_size("row")
    row_tiles = row_span // tile_size
    col_tiles = col_span // tile_size
    block_slots = slot_count // PER_ROW
    live_mask = (jnp.arange(slot_count, dtype=jnp.int32) < live_count).astype(jnp.float32)
    row_weight = jnp.sum(tile_blocks, axis=2, dtype=jnp.float32) * live_mask[:, None]
    col_weight = jnp.sum(tile_blocks, axis=1, dtype=jnp.float32) * live_mask[:, None]
    row_degree_part = (
        jnp.zeros((row_tiles, tile_size), jnp.float32)
        .at[row_tile_ids]
        .add(row_weight)
        .reshape(1, row_span)
    )
    col_degree_part = (
        jnp.zeros((col_tiles, tile_size), jnp.float32)
        .at[col_tile_ids]
        .add(col_weight)
        .reshape(1, col_span)
    )

    def to_rows(partial_value):
        return lax.psum_scatter(partial_value, "col", scatter_dimension=1, tiled=True)

    def to_cols(partial_value):
        return lax.psum_scatter(partial_value, "row", scatter_dimension=1, tiled=True)

    degree = 0.5 * (to_rows(row_degree_part) + to_cols(col_degree_part))

    def inner_sums(parts):
        return lax.psum(parts, ("row", "col"))

    solution = jnp.zeros_like(scores)
    residual = scores
    direction = scores
    norm_now = inner_sums(jnp.sum(residual * residual, axis=1))
    for step_index in range(ITERS):
        graph_own_low = direction.astype(jnp.bfloat16)
        graph_col_dir = lax.all_gather(graph_own_low, "row", axis=1, tiled=True)
        graph_row_dir = lax.all_gather(graph_own_low, "col", axis=1, tiled=True)
        col_blocks = graph_col_dir.reshape(task_count, col_tiles, tile_size)
        row_blocks = graph_row_dir.reshape(task_count, row_tiles, tile_size)
        block_count = (live_count + block_slots - 1) // block_slots

        def one_block(block_index, totals):
            forward_sum, backward_sum = totals
            first_slot = block_index * block_slots
            tiles_here = lax.dynamic_slice_in_dim(tile_blocks, first_slot, block_slots, 0)
            rows_here = lax.dynamic_slice_in_dim(row_tile_ids, first_slot, block_slots, 0)
            cols_here = lax.dynamic_slice_in_dim(col_tile_ids, first_slot, block_slots, 0)
            live_here = (first_slot + jnp.arange(block_slots, dtype=jnp.int32) < live_count).astype(
                jnp.float32
            )
            col_pieces = jnp.take(col_blocks, cols_here, axis=1)
            row_pieces = jnp.take(row_blocks, rows_here, axis=1)
            forward = (
                jnp.einsum(
                    "ksd,sod->kso", col_pieces, tiles_here, preferred_element_type=jnp.float32
                )
                * live_here[None, :, None]
            )
            backward = (
                jnp.einsum(
                    "kso,sod->ksd", row_pieces, tiles_here, preferred_element_type=jnp.float32
                )
                * live_here[None, :, None]
            )
            return (
                forward_sum.at[:, rows_here, :].add(forward),
                backward_sum.at[:, cols_here, :].add(backward),
            )

        empty_sums = (
            jnp.zeros((task_count, row_tiles, tile_size), jnp.float32),
            jnp.zeros((task_count, col_tiles, tile_size), jnp.float32),
        )
        forward_sum, backward_sum = lax.fori_loop(0, block_count, one_block, empty_sums)
        forward_part = forward_sum.reshape(task_count, row_span)
        backward_part = backward_sum.reshape(task_count, col_span)
        image_field = direction + coupling * (
            degree * direction - 0.5 * (to_rows(forward_part) + to_cols(backward_part))
        )
        curvature = inner_sums(jnp.sum(direction * image_field, axis=1))
        step_size = norm_now / curvature
        solution = solution + step_size[:, None] * direction
        residual = residual - step_size[:, None] * image_field
        if step_index + 1 < ITERS:
            norm_next = inner_sums(jnp.sum(residual * residual, axis=1))
            direction = residual + (norm_next / norm_now)[:, None] * direction
            norm_now = norm_next
    return (solution, residual)


def solution(mesh):
    return jax.shard_map(
        per_device,
        mesh=mesh,
        in_specs=(
            P(None, ("row", "col")),
            P("row", "col", None, None, None),
            P("row", "col", None),
            P("row", "col", None),
            P("row", "col"),
        ),
        out_specs=(P(None, ("row", "col")), P(None, ("row", "col"))),
        check_vma=False,
    )
```

profile of v0, /device:TPU:1, one launch (start us, length us, event | category | flops | bytes accessed | tf_op | source)
XLA Modules:
  0.0 1218.0 jit_solution(540083142210740069)
XLA Ops:
  7.9 9.8 convert_reduce_fusion
  26.0 4.0 copy.53
  30.8 23.3 %all_gather.19 = bf16[32,12288]{1,0:T(8,128)(2,1)S(1)} all-gather(bf16[32,768]{1,0:T(8,128)(2,1)S(1)} %convert_element_type.43), channel_id=1, replica_groups=mesh['row'=8,'col'=16] {'col'}, dimensions={1}, use_global_device_ids=true | all-gather | bytes 835584 | tf_op jit(solution)/shard_map/all_gather | solution.py:59
  54.2 17.6 %all_gather.18 = bf16[32,6144]{1,0:T(8,128)(2,1)S(1)} all-gather(bf16[32,768]{1,0:T(8,128)(2,1)S(1)} %convert_element_type.43), channel_id=1, replica_groups=mesh['row'=8,'col'=16] {'row'}, dimensions={1}, use_global_device_ids=true | all-gather | bytes 442368 | tf_op jit(solution)/shard_map/all_gather | solution.py:58
  74.4 137.2 %while.36 = (s32[]{:T(128)}, f32[32,96,128]{2,0,1:T(8,128)}, f32[32,48,128]{2,0,1:T(8,128)S(1)}, s32[]{:T(128)}, s32[480]{0:T(512)}, /*index=5*/bf16[480,128,128...) while((s32[]{:T(128)}, f32[32,96,128]{2,0,1:T(8,128)}, ...), condition=%wide.region_11.14_spmd, body=%wide.region_8.13_spmd.sunk | while | flops 203689376 | bytes 23607144 | solution.py:96
  77.1 3.7 multiply_bitcast_fusion.12
  80.8 11.9 scatter_fusion
  97.4 4.4 scatter_fusion.1
  104.6 3.8 multiply_bitcast_fusion.12
  108.4 11.8 scatter_fusion
  125.0 4.5 scatter_fusion.1
  132.2 3.7 multiply_bitcast_fusion.12
  135.9 11.8 scatter_fusion
  152.5 4.4 scatter_fusion.1
  159.6 3.7 multiply_bitcast_fusion.12
  163.3 11.8 scatter_fusion
  179.8 4.4 scatter_fusion.1
  187.0 3.7 multiply_bitcast_fusion.12
  190.6 11.8 scatter_fusion
  207.2 4.4 scatter_fusion.1
  217.0 22.7 %reduce-scatter.15.cloned.1.call-done = f32[32,768]{1,0:T(8,128)} async-done(((f32[32,6144]{1,0:T(8,128)}), f32[32,768]{1,0:T(8,128)}) %reduce-scatter.15.cloned.1.call-update) | async-done | bytes 98320 | tf_op jit(solution)/shard_map/reduce_scatter | solution.py:45
  239.7 77.5 %reduce-scatter.13.cloned.1.call-done = f32[32,768]{1,0:T(8,128)} async-done(((f32[32,12288]{1,0:T(8,128)}), f32[32,768]{1,0:T(8,128)}) %reduce-scatter.13.cloned.1.call-update) | async-done | bytes 98320 | tf_op jit(solution)/shard_map/reduce_scatter | solution.py:42
  318.3 66.1 %all-reduce = (f32[32]{0:T(128)S(1)}, f32[32]{0:T(128)S(1)}) all-reduce(f32[32]{0:T(128)S(1)} %get-tuple-element.255, f32[32]{0:T(128)S(1)} %get-tuple-element.254), channel_id=1, replica_groups=mesh['row'=8,'col'=16] {'row','col'}, use_global_device_ids=true, to_apply=%region_1.0 | all-reduce | flops 64 | bytes 512 | tf_op jit(solution)/shard_map/psum | solution.py:50
  385.5 62.5 %psum.44 = f32[32]{0:T(128)S(1)} all-reduce(f32[32]{0:T(128)S(1)} %get-tuple-element.334), channel_id=1, replica_groups=mesh['row'=8,'col'=16] {'row','col'}, use_global_device_ids=true, to_apply=%region_17.20 | all-reduce | flops 32 | bytes 256 | tf_op jit(solution)/shard_map/psum | solution.py:50
  448.8 19.0 %all_gather.21 = bf16[32,12288]{1,0:T(8,128)(2,1)S(1)} all-gather(bf16[32,768]{1,0:T(8,128)(2,1)S(1)} %get-tuple-element.332), channel_id=1, replica_groups=mesh['row'=8,'col'=16] {'col'}, dimensions={1}, use_global_device_ids=true | all-gather | bytes 835584 | tf_op jit(solution)/shard_map/all_gather | solution.py:59
  467.8 18.5 %all_gather.20 = bf16[32,6144]{1,0:T(8,128)(2,1)S(1)} all-gather(bf16[32,768]{1,0:T(8,128)(2,1)S(1)} %get-tuple-element.332), channel_id=1, replica_groups=mesh['row'=8,'col'=16] {'row'}, dimensions={1}, use_global_device_ids=true | all-gather | bytes 442368 | tf_op jit(solution)/shard_map/all_gather | solution.py:58
  488.9 137.0 %while.37 = (s32[]{:T(128)}, f32[32,96,128]{2,0,1:T(8,128)}, f32[32,48,128]{2,0,1:T(8,128)S(1)}, s32[]{:T(128)}, s32[480]{0:T(512)}, /*index=5*/bf16[480,128,128...) while((s32[]{:T(128)}, f32[32,96,128]{2,0,1:T(8,128)}, ...), condition=%wide.region_21.24_spmd, body=%wide.region_18.23_spmd.sunk | while | flops 203689376 | bytes 23607556 | solution.py:96
  491.6 3.7 multiply_bitcast_fusion.14
  495.3 11.8 scatter_fusion.2
  511.8 4.4 scatter_fusion.3
  519.0 3.7 multiply_bitcast_fusion.14
  522.6 11.8 scatter_fusion.2
  539.2 4.5 scatter_fusion.3
  546.4 3.7 multiply_bitcast_fusion.14
  550.0 11.8 scatter_fusion.2
  566.6 4.4 scatter_fusion.3
  573.7 3.7 multiply_bitcast_fusion.14
  577.4 11.8 scatter_fusion.2
  594.0 4.4 scatter_fusion.3
  601.1 3.7 multiply_bitcast_fusion.14
  604.8 11.8 scatter_fusion.2
  621.4 4.4 scatter_fusion.3
  628.9 23.5 %reduce-scatter.19.cloned.1.call-done = f32[32,768]{1,0:T(8,128)} async-done(((f32[32,6144]{1,0:T(8,128)}), f32[32,768]{1,0:T(8,128)}) %reduce-scatter.19.cloned.1.call-update) | async-done | bytes 98320 | tf_op jit(solution)/shard_map/reduce_scatter | solution.py:45
  652.3 77.6 %reduce-scatter.17.cloned.1.call-done = f32[32,768]{1,0:T(8,128)} async-done(((f32[32,12288]{1,0:T(8,128)}), f32[32,768]{1,0:T(8,128)}) %reduce-scatter.17.cloned.1.call-update) | async-done | bytes 98320 | tf_op jit(solution)/shard_map/reduce_scatter | solution.py:42
  731.0 65.9 %psum.45 = f32[32]{0:T(128)S(1)} all-reduce(f32[32]{0:T(128)S(1)} %multiply_reduce_fusion.2), channel_id=1, replica_groups=mesh['row'=8,'col'=16] {'row','col'}, use_global_device_ids=true, to_apply=%region_25.28 | all-reduce | flops 32 | bytes 256 | tf_op jit(solution)/shard_map/psum | solution.py:50
  798.1 62.5 %psum.46 = f32[32]{0:T(128)S(1)} all-reduce(f32[32]{0:T(128)S(1)} %get-tuple-element.330), channel_id=1, replica_groups=mesh['row'=8,'col'=16] {'row','col'}, use_global_device_ids=true, to_apply=%region_27.30 | all-reduce | flops 32 | bytes 256 | tf_op jit(solution)/shard_map/psum | solution.py:50
  860.7 19.0 %all_gather.23 = bf16[32,12288]{1,0:T(8,128)(2,1)S(1)} all-gather(bf16[32,768]{1,0:T(8,128)(2,1)S(1)} %fusion.69), channel_id=1, replica_groups=mesh['row'=8,'col'=16] {'col'}, dimensions={1}, use_global_device_ids=true | all-gather | bytes 835584 | tf_op jit(solution)/shard_map/all_gather | solution.py:59
  879.7 18.8 %all_gather.22 = bf16[32,6144]{1,0:T(8,128)(2,1)S(1)} all-gather(bf16[32,768]{1,0:T(8,128)(2,1)S(1)} %fusion.69), channel_id=1, replica_groups=mesh['row'=8,'col'=16] {'row'}, dimensions={1}, use_global_device_ids=true | all-gather | bytes 442368 | tf_op jit(solution)/shard_map/all_gather | solution.py:58
  901.0 137.0 %while.38 = (s32[]{:T(128)}, f32[32,96,128]{2,0,1:T(8,128)}, f32[32,48,128]{2,0,1:T(8,128)S(1)}, s32[]{:T(128)}, s32[480]{0:T(512)}, /*index=5*/bf16[480,128,128...) while((s32[]{:T(128)}, f32[32,96,128]{2,0,1:T(8,128)}, ...), condition=%wide.region_31.34_spmd, body=%wide.region_28.33_spmd.sunk | while | flops 203689376 | bytes 23607556 | solution.py:96
  903.7 3.7 multiply_bitcast_fusion.16
  907.4 11.8 scatter_fusion.4
  924.0 4.4 scatter_fusion.5
  934.8 11.8 scatter_fusion.4
  951.3 4.5 scatter_fusion.5
  958.5 3.7 multiply_bitcast_fusion.16
  962.2 11.8 scatter_fusion.4
  978.7 4.4 scatter_fusion.5
  989.6 11.8 scatter_fusion.4
  1006.1 4.4 scatter_fusion.5
  1017.0 11.8 scatter_fusion.4
  1033.5 4.4 scatter_fusion.5
  1041.0 23.5 %reduce-scatter.23.cloned.1.call-done = f32[32,768]{1,0:T(8,128)} async-done(((f32[32,6144]{1,0:T(8,128)}), f32[32,768]{1,0:T(8,128)}) %reduce-scatter.23.cloned.1.call-update) | async-done | bytes 98320 | tf_op jit(solution)/shard_map/reduce_scatter | solution.py:45
  1064.5 77.8 %reduce-scatter.21.cloned.1.call-done = f32[32,768]{1,0:T(8,128)} async-done(((f32[32,12288]{1,0:T(8,128)}), f32[32,768]{1,0:T(8,128)}) %reduce-scatter.21.cloned.1.call-update) | async-done | bytes 98320 | tf_op jit(solution)/shard_map/reduce_scatter | solution.py:42
  1143.4 65.9 %psum.47 = f32[32]{0:T(128)S(1)} all-reduce(f32[32]{0:T(128)S(1)} %multiply_reduce_fusion), channel_id=1, replica_groups=mesh['row'=8,'col'=16] {'row','col'}, use_global_device_ids=true, to_apply=%region_35.38 | all-reduce | flops 32 | bytes 256 | tf_op jit(solution)/shard_map/psum | solution.py:50
  (231 shorter events, 158.3 us)
Async XLA Ops:
  7.2 207.5 %reduce-scatter.27.cloned.1.call-start = ((), (), s32[]{:S(2)}) async-start(), calls=%async_computation.15 | async-start | bytes 3538944
  22.9 192.9 %reduce-scatter.25.cloned.1.call-start = ((), (), s32[]{:S(2)}) async-start(), calls=%async_computation.14 | async-start | bytes 6684672
  29.9 0.9 copy-start.5
  30.0 209.8 %reduce-scatter.15.cloned.1.call-start = ((), (), s32[]{:S(2)}) async-start(), calls=%async_computation.9 | async-start | bytes 884736 | tf_op jit(solution)/shard_map/reduce_scatter | solution.py:45
  211.6 1.7 copy-start.1
  212.6 104.6 %reduce-scatter.13.cloned.1.call-start = ((), (), s32[]{:S(2)}) async-start(), calls=%async_computation.8 | async-start | bytes 1671168 | tf_op jit(solution)/shard_map/reduce_scatter | solution.py:42
  214.6 102.6 %copy-start.6 = (f32[32,768]{1,0:T(8,128)S(1)}, f32[32,768]{1,0:T(8,128)}, u32[]{:S(2)}) copy-start(f32[32,768]{1,0:T(8,128)} %param.15) | copy-start | bytes 294916
  214.6 437.7 %reduce-scatter.19.cloned.1.call-start = ((), (), s32[]{:S(2)}) async-start(), calls=%async_computation.11 | async-start | bytes 884736 | tf_op jit(solution)/shard_map/reduce_scatter | solution.py:45
  384.4 103.0 %copy-start.16 = (f32[32]{0:T(128)}, f32[32]{0:T(128)S(1)}, u32[]{:S(2)}) copy-start(f32[32]{0:T(128)S(1)} %div.22) | copy-start | bytes 388
  385.5 101.8 %copy-start.10 = (f32[32,768]{1,0:T(8,128)}, f32[32,768]{1,0:T(8,128)S(1)}, u32[]{:S(2)}) copy-start(f32[32,768]{1,0:T(8,128)S(1)} %get-tuple-element.335) | copy-start | bytes 294916
  448.0 39.3 %copy-start.20 = (f32[32]{0:T(128)}, f32[32]{0:T(128)S(1)}, u32[]{:S(2)}) copy-start(f32[32]{0:T(128)S(1)} %psum.44) | copy-start | bytes 388
  507.1 1.9 copy-start.12
  534.4 1.9 copy-start.12
  561.8 1.9 copy-start.12
  589.2 1.9 copy-start.12
  616.6 1.9 copy-start.12
  625.8 1.7 copy-start.2
  626.8 103.1 %reduce-scatter.17.cloned.1.call-start = ((), (), s32[]{:S(2)}) async-start(), calls=%async_computation.10 | async-start | bytes 1671168 | tf_op jit(solution)/shard_map/reduce_scatter | solution.py:42
  628.8 101.2 %copy-start.3 = (f32[32,768]{1,0:T(8,128)S(1)}, f32[32,768]{1,0:T(8,128)}, u32[]{:S(2)}) copy-start(f32[32,768]{1,0:T(8,128)} %get-tuple-element.333) | copy-start | bytes 294916
  628.8 168.1 %copy-start.21 = (f32[32]{0:T(128)S(1)}, f32[32]{0:T(128)}, u32[]{:S(2)}) copy-start(f32[32]{0:T(128)} %copy-done.20) | copy-start | bytes 388
  628.8 168.1 %copy-start.11 = (f32[32,768]{1,0:T(8,128)S(1)}, f32[32,768]{1,0:T(8,128)}, u32[]{:S(2)}) copy-start(f32[32,768]{1,0:T(8,128)} %copy-done.10) | copy-start | bytes 294916
  628.8 435.7 %reduce-scatter.23.cloned.1.call-start = ((), (), s32[]{:S(2)}) async-start(), calls=%async_computation.13 | async-start | bytes 884736 | tf_op jit(solution)/shard_map/reduce_scatter | solution.py:45
  796.9 102.6 %copy-start.18 = (f32[32]{0:T(128)}, f32[32]{0:T(128)S(1)}, u32[]{:S(2)}) copy-start(f32[32]{0:T(128)S(1)} %div.24) | copy-start | bytes 388
  798.1 101.5 %copy-start.8 = (f32[32,768]{1,0:T(8,128)}, f32[32,768]{1,0:T(8,128)S(1)}, u32[]{:S(2)}) copy-start(f32[32,768]{1,0:T(8,128)S(1)} %get-tuple-element.331) | copy-start | bytes 294916
  860.6 39.0 %copy-start.22 = (f32[32]{0:T(128)}, f32[32]{0:T(128)S(1)}, u32[]{:S(2)}) copy-start(f32[32]{0:T(128)S(1)} %psum.46) | copy-start | bytes 388
  860.6 39.0 %copy-start.14 = (f32[32]{0:T(128)}, f32[32]{0:T(128)S(1)}, u32[]{:S(2)}) copy-start(f32[32]{0:T(128)S(1)} %div.25) | copy-start | bytes 388
  919.2 1.9 copy-start.13
  946.6 1.9 copy-start.13
  974.0 1.9 copy-start.13
  1001.4 1.9 copy-start.13
  1028.8 1.9 copy-start.13
  1038.0 1.7 copy-start
  1039.0 103.3 %reduce-scatter.21.cloned.1.call-start = ((), (), s32[]{:S(2)}) async-start(), calls=%async_computation.12 | async-start | bytes 1671168 | tf_op jit(solution)/shard_map/reduce_scatter | solution.py:42
  1040.9 101.4 %copy-start.4 = (f32[32,768]{1,0:T(8,128)S(1)}, f32[32,768]{1,0:T(8,128)}, u32[]{:S(2)}) copy-start(f32[32,768]{1,0:T(8,128)} %get-tuple-element.333) | copy-start | bytes 294916
  1040.9 101.4 %copy-start.9 = (f32[32,768]{1,0:T(8,128)S(1)}, f32[32,768]{1,0:T(8,128)}, u32[]{:S(2)}) copy-start(f32[32,768]{1,0:T(8,128)} %copy-done.8) | copy-start | bytes 294916
  1040.9 101.4 %copy-start.15 = (f32[32]{0:T(128)S(1)}, f32[32]{0:T(128)}, u32[]{:S(2)}) copy-start(f32[32]{0:T(128)} %copy-done.14) | copy-start | bytes 388
  1040.9 168.4 %copy-start.23 = (f32[32]{0:T(128)S(1)}, f32[32]{0:T(128)}, u32[]{:S(2)}) copy-start(f32[32]{0:T(128)} %copy-done.22) | copy-start | bytes 388
  1041.0 168.4 %copy-start.7 = (f32[32,768]{1,0:T(8,128)S(1)}, f32[32,768]{1,0:T(8,128)}, u32[]{:S(2)}) copy-start(f32[32,768]{1,0:T(8,128)} %param.15) | copy-start | bytes 294916
  1041.0 168.4 %copy-start.17 = (f32[32]{0:T(128)S(1)}, f32[32]{0:T(128)}, u32[]{:S(2)}) copy-start(f32[32]{0:T(128)} %copy-done.16) | copy-start | bytes 388
  1041.0 168.4 %copy-start.19 = (f32[32]{0:T(128)S(1)}, f32[32]{0:T(128)}, u32[]{:S(2)}) copy-start(f32[32]{0:T(128)} %copy-done.18) | copy-start | bytes 388
Sparse Core Ops, SparseCore 0:
  23.1 36.3 reduce-scatter.26
  62.9 82.0 reduce-scatter.24
  212.7 26.9 reduce-scatter.14
  242.8 74.3 reduce-scatter.12
  626.9 25.3 reduce-scatter.18
  655.4 74.4 reduce-scatter.16
  1039.1 25.3 reduce-scatter.22
  1067.7 74.5 reduce-scatter.20
where the time goes:
time: 1230 us; the launch traced here: 1220 us
  blocking collectives  439 us (36%)
  waiting for transfers between devices  303 us (25%)
  other arithmetic  297 us (24%)
  matrix products  98.6 us (8%)
  local copies, waits for them, and re-layouts  64 us (5%)
  between operations  15.1 us (1%)
    psum x5, blocking collectives, inner_sums(): return lax.psum(parts, ('row', 'col'))  323 us
    reduce_scatter x3, waiting for transfers between devices, to_rows(): lax.psum_scatter(partial_value, 'col', scatter_dimension=1, tiled=True)  233 us
    scatter-add x15, other arithmetic, one_block(): forward_sum.at[:, rows_here, :].add(forward)  177 us
    reduce_scatter x3, waiting for transfers between devices, to_cols(): lax.psum_scatter(partial_value, 'row', scatter_dimension=1, tiled=True)  69.7 us
    scatter-add x15, other arithmetic, one_block(): backward_sum.at[:, cols_here, :].add(backward)  66.7 us
    all_gather x3, blocking collectives, per_device(): graph_row_dir = lax.all_gather(graph_own_low, 'col', axis=1, tiled=True)  61.4 us
    dot_general x15, matrix products, one_block(): jnp.einsum('ksd,sod->kso', col_pieces, tiles_here, preferred_element_type...  55.3 us
    all_gather x3, blocking collectives, per_device(): graph_col_dir = lax.all_gather(graph_own_low, 'row', axis=1, tiled=True)  54.9 us
  transfers between devices with their start and end apart: 8, of which 6 were waited for; matrix products, arithmetic and copies ran while one was open for 13% of the time, Pallas kernels for 0%

commit v1 on v0

--- a/solution.py
+++ b/solution.py
@@ -56,7 +56,9 @@
     for step_index in range(ITERS):
         graph_own_low = direction.astype(jnp.bfloat16)
         graph_col_dir = lax.all_gather(graph_own_low, "row", axis=1, tiled=True)
-        graph_row_dir = lax.all_gather(graph_own_low, "col", axis=1, tiled=True)
+        graph_row_dir = jnp.concatenate(
+            lax.all_to_all(jnp.stack([graph_own_low] * lax.axis_size("col")), "col", 0, 0), axis=1
+        )
         col_blocks = graph_col_dir.reshape(task_count, col_tiles, tile_size)
         row_blocks = graph_row_dir.reshape(task_count, row_tiles, tile_size)
         block_count = (live_count + block_slots - 1) // block_slots

time: 1230 us -> 1190 us (0.967)
  blocking collectives: 439 us -> 365 us
  starting transfers between devices: 0.33 us -> 17.7 us
    all_gather x3 -> x0, blocking collectives: 61.4 us -> none  [per_device(): graph_row_dir = lax.all_gather(graph_own_low, 'col', axis=1, tiled=True)]
    all_to_all x0 -> x3, starting transfers between devices: none -> 17.2 us  [per_device(): lax.all_to_all(jnp.stack([graph_own_low] * lax.axis_size('col')), 'col',...]
    all_gather x3, blocking collectives: 54.9 us -> 41.7 us  [per_device(): graph_col_dir = lax.all_gather(graph_own_low, 'row', axis=1, tiled=True)]
  transfers between devices with their start and end apart: 8 -> 11, of which waited for: 6 -> 6; matrix products, arithmetic and copies ran while one was open for 13% -> 14% of each run, Pallas kernels for 0% -> 0%
where the time goes in v1:
time: 1190 us; the launch traced here: 1180 us
  blocking collectives  365 us (31%)
  waiting for transfers between devices  311 us (26%)
  other arithmetic  299 us (25%)
  matrix products  98.8 us (8%)
  local copies, waits for them, and re-layouts  69.8 us (6%)
  starting transfers between devices  17.7 us (1%)
  between operations  15.1 us (1%)
    psum x5, blocking collectives, inner_sums(): return lax.psum(parts, ('row', 'col'))  323 us
    reduce_scatter x3, waiting for transfers between devices, to_rows(): lax.psum_scatter(partial_value, 'col', scatter_dimension=1, tiled=True)  233 us
    scatter-add x15, other arithmetic, one_block(): forward_sum.at[:, rows_here, :].add(forward)  177 us
    reduce_scatter x3, waiting for transfers between devices, to_cols(): lax.psum_scatter(partial_value, 'row', scatter_dimension=1, tiled=True)  78.7 us
    scatter-add x15, other arithmetic, one_block(): backward_sum.at[:, cols_here, :].add(backward)  66.7 us
    dot_general x15, matrix products, one_block(): jnp.einsum('ksd,sod->kso', col_pieces, tiles_here, preferred_element_type...  55.4 us
    dot_general x15, matrix products, one_block(): jnp.einsum('kso,sod->ksd', row_pieces, tiles_here, preferred_element_type...  43.4 us
    all_gather x3, blocking collectives, per_device(): graph_col_dir = lax.all_gather(graph_own_low, 'row', axis=1, tiled=True)  41.7 us
  transfers between devices with their start and end apart: 11, of which 6 were waited for; matrix products, arithmetic and copies ran while one was open for 14% of the time, Pallas kernels for 0%

profile of v1, /device:TPU:1, one launch (start us, length us, event | category | flops | bytes accessed | tf_op | source)
XLA Modules:
  0.0 1177.2 jit_solution(3118179976290717480)
XLA Ops:
  9.0 8.4 all-to-all-start
  18.2 9.8 convert_reduce_fusion
  36.2 4.0 copy.54
  40.3 14.3 %all_gather.9 = bf16[32,6144]{1,0:T(8,128)(2,1)S(1)} all-gather(bf16[32,768]{1,0:T(8,128)(2,1)S(1)} %convert_element_type.43), channel_id=1, replica_groups=mesh['row'=8,'col'=16] {'row'}, dimensions={1}, use_global_device_ids=true | all-gather | bytes 442368 | tf_op jit(solution)/shard_map/all_gather | solution.py:58
  58.5 137.4 %while.36 = (s32[]{:T(128)}, f32[32,96,128]{2,0,1:T(8,128)}, f32[32,48,128]{2,0,1:T(8,128)S(1)}, s32[]{:T(128)}, s32[480]{0:T(512)}, /*index=5*/bf16[480,128,128...) while((s32[]{:T(128)}, f32[32,96,128]{2,0,1:T(8,128)}, ...), condition=%wide.region_11.14_spmd, body=%wide.region_8.13_spmd.sunk | while | flops 203689376 | bytes 23607144 | solution.py:98
  61.2 3.7 multiply_bitcast_fusion.12
  64.9 11.8 %scatter_fusion = f32[32,96,128]{2,0,1:T(8,128)} fusion(f32[32,96,128]{2,0,1:T(8,128)} %get-tuple-element.569, s32[96]{0:T(128)S(1)} %get-tuple-element.522, f32[96,32,128]{2,1,0:T(8,128)S(1)} %multiply_bitcast_fusion.12), kind=kCustom, calls=%fused_computation.6.clone.1 | custom fusion | flops 393216 | bytes 4718976 | tf_op jit(solution)/shard_map/while/body/scatter-add | solution.py:90
  81.5 4.4 scatter_fusion.1
  88.6 3.7 multiply_bitcast_fusion.12
  92.4 11.9 %scatter_fusion = f32[32,96,128]{2,0,1:T(8,128)} fusion(f32[32,96,128]{2,0,1:T(8,128)} %get-tuple-element.569, s32[96]{0:T(128)S(1)} %get-tuple-element.522, f32[96,32,128]{2,1,0:T(8,128)S(1)} %multiply_bitcast_fusion.12), kind=kCustom, calls=%fused_computation.6.clone.1 | custom fusion | flops 393216 | bytes 4718976 | tf_op jit(solution)/shard_map/while/body/scatter-add | solution.py:90
  109.1 4.5 scatter_fusion.1
  116.3 3.8 multiply_bitcast_fusion.12
  120.1 11.8 %scatter_fusion = f32[32,96,128]{2,0,1:T(8,128)} fusion(f32[32,96,128]{2,0,1:T(8,128)} %get-tuple-element.569, s32[96]{0:T(128)S(1)} %get-tuple-element.522, f32[96,32,128]{2,1,0:T(8,128)S(1)} %multiply_bitcast_fusion.12), kind=kCustom, calls=%fused_computation.6.clone.1 | custom fusion | flops 393216 | bytes 4718976 | tf_op jit(solution)/shard_map/while/body/scatter-add | solution.py:90
  136.7 4.4 scatter_fusion.1
  143.8 3.7 multiply_bitcast_fusion.12
  147.5 11.8 %scatter_fusion = f32[32,96,128]{2,0,1:T(8,128)} fusion(f32[32,96,128]{2,0,1:T(8,128)} %get-tuple-element.569, s32[96]{0:T(128)S(1)} %get-tuple-element.522, f32[96,32,128]{2,1,0:T(8,128)S(1)} %multiply_bitcast_fusion.12), kind=kCustom, calls=%fused_computation.6.clone.1 | custom fusion | flops 393216 | bytes 4718976 | tf_op jit(solution)/shard_map/while/body/scatter-add | solution.py:90
  164.1 4.4 scatter_fusion.1
  171.2 3.7 multiply_bitcast_fusion.12
  174.9 11.8 %scatter_fusion = f32[32,96,128]{2,0,1:T(8,128)} fusion(f32[32,96,128]{2,0,1:T(8,128)} %get-tuple-element.569, s32[96]{0:T(128)S(1)} %get-tuple-element.522, f32[96,32,128]{2,1,0:T(8,128)S(1)} %multiply_bitcast_fusion.12), kind=kCustom, calls=%fused_computation.6.clone.1 | custom fusion | flops 393216 | bytes 4718976 | tf_op jit(solution)/shard_map/while/body/scatter-add | solution.py:90
  191.4 4.4 scatter_fusion.1
  201.2 25.4 %reduce-scatter.15.cloned.1.call-done = f32[32,768]{1,0:T(8,128)} async-done(((f32[32,6144]{1,0:T(8,128)}), f32[32,768]{1,0:T(8,128)}) %reduce-scatter.15.cloned.1.call-update) | async-done | bytes 98320 | tf_op jit(solution)/shard_map/reduce_scatter | solution.py:45
  226.6 77.5 %reduce-scatter.13.cloned.1.call-done = f32[32,768]{1,0:T(8,128)} async-done(((f32[32,12288]{1,0:T(8,128)}), f32[32,768]{1,0:T(8,128)}) %reduce-scatter.13.cloned.1.call-update) | async-done | bytes 98320 | tf_op jit(solution)/shard_map/reduce_scatter | solution.py:42
  305.2 65.9 %all-reduce = (f32[32]{0:T(128)S(1)}, f32[32]{0:T(128)S(1)}) all-reduce(f32[32]{0:T(128)S(1)} %get-tuple-element.255, f32[32]{0:T(128)S(1)} %get-tuple-element.254), channel_id=1, replica_groups=mesh['row'=8,'col'=16] {'row','col'}, use_global_device_ids=true, to_apply=%region_1.0 | all-reduce | flops 64 | bytes 512 | tf_op jit(solution)/shard_map/psum | solution.py:50
  372.3 62.5 %psum.44 = f32[32]{0:T(128)S(1)} all-reduce(f32[32]{0:T(128)S(1)} %get-tuple-element.334), channel_id=1, replica_groups=mesh['row'=8,'col'=16] {'row','col'}, use_global_device_ids=true, to_apply=%region_17.20 | all-reduce | flops 32 | bytes 256 | tf_op jit(solution)/shard_map/psum | solution.py:50
  436.5 4.4 all-to-all-start.1
  440.9 13.7 %all_gather.10 = bf16[32,6144]{1,0:T(8,128)(2,1)S(1)} all-gather(bf16[32,768]{1,0:T(8,128)(2,1)S(1)} %get-tuple-element.332), channel_id=1, replica_groups=mesh['row'=8,'col'=16] {'row'}, dimensions={1}, use_global_device_ids=true | all-gather | bytes 442368 | tf_op jit(solution)/shard_map/all_gather | solution.py:58
  458.5 137.3 %while.37 = (s32[]{:T(128)}, f32[32,96,128]{2,0,1:T(8,128)}, f32[32,48,128]{2,0,1:T(8,128)S(1)}, s32[]{:T(128)}, s32[480]{0:T(512)}, /*index=5*/bf16[480,128,128...) while((s32[]{:T(128)}, f32[32,96,128]{2,0,1:T(8,128)}, ...), condition=%wide.region_21.24_spmd, body=%wide.region_18.23_spmd.sunk | while | flops 203689376 | bytes 23607556 | solution.py:98
  461.3 3.7 multiply_bitcast_fusion.14
  465.0 11.8 %scatter_fusion.2 = f32[32,96,128]{2,0,1:T(8,128)} fusion(f32[32,96,128]{2,0,1:T(8,128)} %get-tuple-element.611, s32[96]{0:T(128)S(1)} %get-tuple-element.536, f32[96,32,128]{2,1,0:T(8,128)S(1)} %multiply_bitcast_fusion.14), kind=kCustom, calls=%fused_computation.8.clone.1 | custom fusion | flops 393216 | bytes 4718976 | tf_op jit(solution)/shard_map/while/body/scatter-add | solution.py:90
  481.5 4.4 scatter_fusion.3
  488.7 3.7 multiply_bitcast_fusion.14
  492.4 11.8 %scatter_fusion.2 = f32[32,96,128]{2,0,1:T(8,128)} fusion(f32[32,96,128]{2,0,1:T(8,128)} %get-tuple-element.611, s32[96]{0:T(128)S(1)} %get-tuple-element.536, f32[96,32,128]{2,1,0:T(8,128)S(1)} %multiply_bitcast_fusion.14), kind=kCustom, calls=%fused_computation.8.clone.1 | custom fusion | flops 393216 | bytes 4718976 | tf_op jit(solution)/shard_map/while/body/scatter-add | solution.py:90
  509.0 4.5 scatter_fusion.3
  516.2 3.7 multiply_bitcast_fusion.14
  519.9 11.8 %scatter_fusion.2 = f32[32,96,128]{2,0,1:T(8,128)} fusion(f32[32,96,128]{2,0,1:T(8,128)} %get-tuple-element.611, s32[96]{0:T(128)S(1)} %get-tuple-element.536, f32[96,32,128]{2,1,0:T(8,128)S(1)} %multiply_bitcast_fusion.14), kind=kCustom, calls=%fused_computation.8.clone.1 | custom fusion | flops 393216 | bytes 4718976 | tf_op jit(solution)/shard_map/while/body/scatter-add | solution.py:90
  536.4 4.4 scatter_fusion.3
  543.7 3.7 multiply_bitcast_fusion.14
  547.3 11.8 %scatter_fusion.2 = f32[32,96,128]{2,0,1:T(8,128)} fusion(f32[32,96,128]{2,0,1:T(8,128)} %get-tuple-element.611, s32[96]{0:T(128)S(1)} %get-tuple-element.536, f32[96,32,128]{2,1,0:T(8,128)S(1)} %multiply_bitcast_fusion.14), kind=kCustom, calls=%fused_computation.8.clone.1 | custom fusion | flops 393216 | bytes 4718976 | tf_op jit(solution)/shard_map/while/body/scatter-add | solution.py:90
  563.9 4.4 scatter_fusion.3
  571.1 3.7 multiply_bitcast_fusion.14
  574.8 11.8 %scatter_fusion.2 = f32[32,96,128]{2,0,1:T(8,128)} fusion(f32[32,96,128]{2,0,1:T(8,128)} %get-tuple-element.611, s32[96]{0:T(128)S(1)} %get-tuple-element.536, f32[96,32,128]{2,1,0:T(8,128)S(1)} %multiply_bitcast_fusion.14), kind=kCustom, calls=%fused_computation.8.clone.1 | custom fusion | flops 393216 | bytes 4718976 | tf_op jit(solution)/shard_map/while/body/scatter-add | solution.py:90
  591.3 4.4 scatter_fusion.3
  598.8 26.7 %reduce-scatter.19.cloned.1.call-done = f32[32,768]{1,0:T(8,128)} async-done(((f32[32,6144]{1,0:T(8,128)}), f32[32,768]{1,0:T(8,128)}) %reduce-scatter.19.cloned.1.call-update) | async-done | bytes 98320 | tf_op jit(solution)/shard_map/reduce_scatter | solution.py:45
  625.5 77.5 %reduce-scatter.17.cloned.1.call-done = f32[32,768]{1,0:T(8,128)} async-done(((f32[32,12288]{1,0:T(8,128)}), f32[32,768]{1,0:T(8,128)}) %reduce-scatter.17.cloned.1.call-update) | async-done | bytes 98320 | tf_op jit(solution)/shard_map/reduce_scatter | solution.py:42
  704.1 65.9 %psum.45 = f32[32]{0:T(128)S(1)} all-reduce(f32[32]{0:T(128)S(1)} %multiply_reduce_fusion.2), channel_id=1, replica_groups=mesh['row'=8,'col'=16] {'row','col'}, use_global_device_ids=true, to_apply=%region_25.28 | all-reduce | flops 32 | bytes 256 | tf_op jit(solution)/shard_map/psum | solution.py:50
  771.1 62.7 %psum.46 = f32[32]{0:T(128)S(1)} all-reduce(f32[32]{0:T(128)S(1)} %get-tuple-element.330), channel_id=1, replica_groups=mesh['row'=8,'col'=16] {'row','col'}, use_global_device_ids=true, to_apply=%region_27.30 | all-reduce | flops 32 | bytes 256 | tf_op jit(solution)/shard_map/psum | solution.py:50
  834.9 4.4 all-to-all-start.2
  839.4 13.7 %all_gather.11 = bf16[32,6144]{1,0:T(8,128)(2,1)S(1)} all-gather(bf16[32,768]{1,0:T(8,128)(2,1)S(1)} %fusion.69), channel_id=1, replica_groups=mesh['row'=8,'col'=16] {'row'}, dimensions={1}, use_global_device_ids=true | all-gather | bytes 442368 | tf_op jit(solution)/shard_map/all_gather | solution.py:58
  857.0 137.3 %while.38 = (s32[]{:T(128)}, f32[32,96,128]{2,0,1:T(8,128)}, f32[32,48,128]{2,0,1:T(8,128)S(1)}, s32[]{:T(128)}, s32[480]{0:T(512)}, /*index=5*/bf16[480,128,128...) while((s32[]{:T(128)}, f32[32,96,128]{2,0,1:T(8,128)}, ...), condition=%wide.region_31.34_spmd, body=%wide.region_28.33_spmd.sunk | while | flops 203689376 | bytes 23607556 | solution.py:98
  859.7 3.7 multiply_bitcast_fusion.16
  863.4 11.8 %scatter_fusion.4 = f32[32,96,128]{2,0,1:T(8,128)} fusion(f32[32,96,128]{2,0,1:T(8,128)} %get-tuple-element.653, s32[96]{0:T(128)S(1)} %get-tuple-element.550, f32[96,32,128]{2,1,0:T(8,128)S(1)} %multiply_bitcast_fusion.16), kind=kCustom, calls=%fused_computation.10.clone.1 | custom fusion | flops 393216 | bytes 4718976 | tf_op jit(solution)/shard_map/while/body/scatter-add | solution.py:90
  880.0 4.4 scatter_fusion.5
  890.9 11.8 %scatter_fusion.4 = f32[32,96,128]{2,0,1:T(8,128)} fusion(f32[32,96,128]{2,0,1:T(8,128)} %get-tuple-element.653, s32[96]{0:T(128)S(1)} %get-tuple-element.550, f32[96,32,128]{2,1,0:T(8,128)S(1)} %multiply_bitcast_fusion.16), kind=kCustom, calls=%fused_computation.10.clone.1 | custom fusion | flops 393216 | bytes 4718976 | tf_op jit(solution)/shard_map/while/body/scatter-add | solution.py:90
  907.4 4.5 scatter_fusion.5
  914.7 3.7 multiply_bitcast_fusion.16
  918.3 11.8 %scatter_fusion.4 = f32[32,96,128]{2,0,1:T(8,128)} fusion(f32[32,96,128]{2,0,1:T(8,128)} %get-tuple-element.653, s32[96]{0:T(128)S(1)} %get-tuple-element.550, f32[96,32,128]{2,1,0:T(8,128)S(1)} %multiply_bitcast_fusion.16), kind=kCustom, calls=%fused_computation.10.clone.1 | custom fusion | flops 393216 | bytes 4718976 | tf_op jit(solution)/shard_map/while/body/scatter-add | solution.py:90
  934.9 4.4 scatter_fusion.5
  945.8 11.8 %scatter_fusion.4 = f32[32,96,128]{2,0,1:T(8,128)} fusion(f32[32,96,128]{2,0,1:T(8,128)} %get-tuple-element.653, s32[96]{0:T(128)S(1)} %get-tuple-element.550, f32[96,32,128]{2,1,0:T(8,128)S(1)} %multiply_bitcast_fusion.16), kind=kCustom, calls=%fused_computation.10.clone.1 | custom fusion | flops 393216 | bytes 4718976 | tf_op jit(solution)/shard_map/while/body/scatter-add | solution.py:90
  962.3 4.4 scatter_fusion.5
  973.2 11.8 %scatter_fusion.4 = f32[32,96,128]{2,0,1:T(8,128)} fusion(f32[32,96,128]{2,0,1:T(8,128)} %get-tuple-element.653, s32[96]{0:T(128)S(1)} %get-tuple-element.550, f32[96,32,128]{2,1,0:T(8,128)S(1)} %multiply_bitcast_fusion.16), kind=kCustom, calls=%fused_computation.10.clone.1 | custom fusion | flops 393216 | bytes 4718976 | tf_op jit(solution)/shard_map/while/body/scatter-add | solution.py:90
  989.8 4.4 scatter_fusion.5
  997.3 26.6 %reduce-scatter.23.cloned.1.call-done = f32[32,768]{1,0:T(8,128)} async-done(((f32[32,6144]{1,0:T(8,128)}), f32[32,768]{1,0:T(8,128)}) %reduce-scatter.23.cloned.1.call-update) | async-done | bytes 98320 | tf_op jit(solution)/shard_map/reduce_scatter | solution.py:45
  1023.9 77.6 %reduce-scatter.21.cloned.1.call-done = f32[32,768]{1,0:T(8,128)} async-done(((f32[32,12288]{1,0:T(8,128)}), f32[32,768]{1,0:T(8,128)}) %reduce-scatter.21.cloned.1.call-update) | async-done | bytes 98320 | tf_op jit(solution)/shard_map/reduce_scatter | solution.py:42
  1102.7 65.9 %psum.47 = f32[32]{0:T(128)S(1)} all-reduce(f32[32]{0:T(128)S(1)} %multiply_reduce_fusion), channel_id=1, replica_groups=mesh['row'=8,'col'=16] {'row','col'}, use_global_device_ids=true, to_apply=%region_35.38 | all-reduce | flops 32 | bytes 256 | tf_op jit(solution)/shard_map/psum | solution.py:50
  (241 shorter events, 166.0 us)
Async XLA Ops:
  9.0 45.7 %all-to-all-start = ((bf16[16,32,768]{2,1,0:T(8,128)(2,1)}), bf16[16,32,768]{2,1,0:T(8,128)(2,1)S(1)}, u32[]{:S(2)}, u32[]{:S(2)}) async-start(bf16[16,32,768]{2,1,0:T(8,128)(2,1)} %stack.6), calls=%async_computation | async-start | bytes 1572864 | tf_op jit(solution)/shard_map/all_to_all | solution.py:60
  17.5 181.5 %reduce-scatter.27.cloned.1.call-start = ((), (), s32[]{:S(2)}) async-start(), calls=%async_computation.18 | async-start | bytes 3538944
  33.2 166.8 %reduce-scatter.25.cloned.1.call-start = ((), (), s32[]{:S(2)}) async-start(), calls=%async_computation.17 | async-start | bytes 6684672
  40.3 186.4 %reduce-scatter.15.cloned.1.call-start = ((), (), s32[]{:S(2)}) async-start(), calls=%async_computation.12 | async-start | bytes 884736 | tf_op jit(solution)/shard_map/reduce_scatter | solution.py:45
  195.9 1.7 copy-start.1
  196.9 107.2 %reduce-scatter.13.cloned.1.call-start = ((), (), s32[]{:S(2)}) async-start(), calls=%async_computation.11 | async-start | bytes 1671168 | tf_op jit(solution)/shard_map/reduce_scatter | solution.py:42
  198.9 105.3 %copy-start.5 = (f32[32,768]{1,0:T(8,128)S(1)}, f32[32,768]{1,0:T(8,128)}, u32[]{:S(2)}) copy-start(f32[32,768]{1,0:T(8,128)} %param.15) | copy-start | bytes 294916
  371.1 65.3 %copy-start.15 = (f32[32]{0:T(128)}, f32[32]{0:T(128)S(1)}, u32[]{:S(2)}) copy-start(f32[32]{0:T(128)S(1)} %div.22) | copy-start | bytes 388
  372.3 64.2 %copy-start.9 = (f32[32,768]{1,0:T(8,128)}, f32[32,768]{1,0:T(8,128)S(1)}, u32[]{:S(2)}) copy-start(f32[32,768]{1,0:T(8,128)S(1)} %get-tuple-element.335) | copy-start | bytes 294916
  434.8 1.7 copy-start.19
  436.5 18.3 %all-to-all-start.1 = ((bf16[16,32,768]{2,1,0:T(8,128)(2,1)}), bf16[16,32,768]{2,1,0:T(8,128)(2,1)S(1)}, u32[]{:S(2)}, u32[]{:S(2)}) async-start(bf16[16,32,768]{2,1,0:T(8,128)(2,1)} %stack.7), calls=%async_computation.3 | async-start | bytes 1572864 | tf_op jit(solution)/shard_map/all_to_all | solution.py:60
  440.9 184.6 %reduce-scatter.19.cloned.1.call-start = ((), (), s32[]{:S(2)}) async-start(), calls=%async_computation.14 | async-start | bytes 884736 | tf_op jit(solution)/shard_map/reduce_scatter | solution.py:45
  476.8 1.9 copy-start.11
  504.2 1.9 copy-start.11
  531.7 1.9 copy-start.11
  559.1 1.9 copy-start.11
  586.6 1.9 copy-start.11
  595.8 1.7 copy-start.2
  596.8 106.2 %reduce-scatter.17.cloned.1.call-start = ((), (), s32[]{:S(2)}) async-start(), calls=%async_computation.13 | async-start | bytes 1671168 | tf_op jit(solution)/shard_map/reduce_scatter | solution.py:42
  598.8 104.2 %copy-start.3 = (f32[32,768]{1,0:T(8,128)S(1)}, f32[32,768]{1,0:T(8,128)}, u32[]{:S(2)}) copy-start(f32[32,768]{1,0:T(8,128)} %get-tuple-element.333) | copy-start | bytes 294916
  598.8 171.2 %copy-start.20 = (f32[32]{0:T(128)S(1)}, f32[32]{0:T(128)}, u32[]{:S(2)}) copy-start(f32[32]{0:T(128)} %copy-done.19) | copy-start | bytes 388
  598.8 171.2 %copy-start.10 = (f32[32,768]{1,0:T(8,128)S(1)}, f32[32,768]{1,0:T(8,128)}, u32[]{:S(2)}) copy-start(f32[32,768]{1,0:T(8,128)} %copy-done.9) | copy-start | bytes 294916
  770.0 64.9 %copy-start.17 = (f32[32]{0:T(128)}, f32[32]{0:T(128)S(1)}, u32[]{:S(2)}) copy-start(f32[32]{0:T(128)S(1)} %div.24) | copy-start | bytes 388
  771.1 63.8 %copy-start.7 = (f32[32,768]{1,0:T(8,128)}, f32[32,768]{1,0:T(8,128)S(1)}, u32[]{:S(2)}) copy-start(f32[32,768]{1,0:T(8,128)S(1)} %get-tuple-element.331) | copy-start | bytes 294916
  833.9 1.1 copy-start.21
  833.9 1.1 copy-start.13
  834.9 18.3 %all-to-all-start.2 = ((bf16[16,32,768]{2,1,0:T(8,128)(2,1)}), bf16[16,32,768]{2,1,0:T(8,128)(2,1)S(1)}, u32[]{:S(2)}, u32[]{:S(2)}) async-start(bf16[16,32,768]{2,1,0:T(8,128)(2,1)} %stack.8), calls=%async_computation.6 | async-start | bytes 1572864 | tf_op jit(solution)/shard_map/all_to_all | solution.py:60
  839.3 184.6 %reduce-scatter.23.cloned.1.call-start = ((), (), s32[]{:S(2)}) async-start(), calls=%async_computation.16 | async-start | bytes 884736 | tf_op jit(solution)/shard_map/reduce_scatter | solution.py:45
  875.2 1.9 copy-start.12
  902.7 1.9 copy-start.12
  930.1 1.9 copy-start.12
  957.6 1.9 copy-start.12
  985.0 1.9 copy-start.12
  994.3 1.7 copy-start
  995.2 106.3 %reduce-scatter.21.cloned.1.call-start = ((), (), s32[]{:S(2)}) async-start(), calls=%async_computation.15 | async-start | bytes 1671168 | tf_op jit(solution)/shard_map/reduce_scatter | solution.py:42
  997.2 104.3 %copy-start.4 = (f32[32,768]{1,0:T(8,128)S(1)}, f32[32,768]{1,0:T(8,128)}, u32[]{:S(2)}) copy-start(f32[32,768]{1,0:T(8,128)} %get-tuple-element.333) | copy-start | bytes 294916
  997.2 104.3 %copy-start.8 = (f32[32,768]{1,0:T(8,128)S(1)}, f32[32,768]{1,0:T(8,128)}, u32[]{:S(2)}) copy-start(f32[32,768]{1,0:T(8,128)} %copy-done.7) | copy-start | bytes 294916
  997.2 104.3 %copy-start.14 = (f32[32]{0:T(128)S(1)}, f32[32]{0:T(128)}, u32[]{:S(2)}) copy-start(f32[32]{0:T(128)} %copy-done.13) | copy-start | bytes 388
  997.2 171.4 %copy-start.22 = (f32[32]{0:T(128)S(1)}, f32[32]{0:T(128)}, u32[]{:S(2)}) copy-start(f32[32]{0:T(128)} %copy-done.21) | copy-start | bytes 388
  997.2 171.4 %copy-start.6 = (f32[32,768]{1,0:T(8,128)S(1)}, f32[32,768]{1,0:T(8,128)}, u32[]{:S(2)}) copy-start(f32[32,768]{1,0:T(8,128)} %param.15) | copy-start | bytes 294916
  997.2 171.4 %copy-start.16 = (f32[32]{0:T(128)S(1)}, f32[32]{0:T(128)}, u32[]{:S(2)}) copy-start(f32[32]{0:T(128)} %copy-done.15) | copy-start | bytes 388
  997.2 171.4 %copy-start.18 = (f32[32]{0:T(128)S(1)}, f32[32]{0:T(128)}, u32[]{:S(2)}) copy-start(f32[32]{0:T(128)} %copy-done.17) | copy-start | bytes 388
Sparse Core Ops, SparseCore 0:
  33.3 35.8 reduce-scatter.26
  72.7 81.7 reduce-scatter.24
  197.0 29.5 reduce-scatter.14
  229.7 74.3 reduce-scatter.12
  596.9 28.5 reduce-scatter.18
  628.6 74.3 reduce-scatter.16
  995.4 28.4 reduce-scatter.22
  1027.1 74.3 reduce-scatter.20
